TPU v7x, 512 devices: a whole 4x8x8 slice. The times are simulated.
512 devices in a mesh: gossip: 16 (over z, y_lo), shard: 32 (over x, y_hi, core).
Axes of the slice: x: 4, y: 8 (y_hi: 4, y_lo: 2; y = y_hi * 2 + y_lo), z: 8, core: 2. Of those that a mesh axis runs over, the one named last changes fastest.
Arguments:
- inputs: bfloat16 [16, 13824, 2020], P('gossip', 'shard'), may hold values from -6 to 6
- upstream: bfloat16 [16, 13824, 1010], P('gossip', 'shard'), may hold values from -6 to 6
- params: float32 [16, 2048, 1010], P('gossip', 'shard'), may hold values from -0.125 to 0.125
- ps_weight: float32 [16], P('gossip'), may hold values from 0.5 to 2
- step: int32 [1], replicated, may hold values from 0 to 999
- cycle_order: int32 [16], replicated, may hold values from 0 to 15, each once
Outputs:
- grad_in: bfloat16 [16, 13824, 2020], P('gossip', 'shard')
- new_params: float32 [16, 2048, 1010], P('gossip', 'shard')
- new_weight: float32 [16], P('gossip')
Inputs may be any that keep to these rules, and one draw needn't show every extreme that they name: cycle_order names every group once.
All inputs are finite; a program needn't handle non-finite values.
Results may differ from a plain program's by a relative error of at most 0.0061.
Values may be sent and summed in bfloat16 or wider, within the bound.
No kernel may reach another device: no remote copies, remote signals or barrier semaphores. Data moves between devices by JAX's collectives and lax.ppermute only.
A program may use at most 64 MiB of HBM per device.

v0:
```python
import jax
import jax.numpy as jnp
from jax import lax
from jax.sharding import PartitionSpec as P

learn_rate = 0.5


def body(inputs, upstream, params, ps_weight, step, cycle_order):
    x_rows = inputs[0]
    up_rows = upstream[0]
    own_shard = params[0]
    weight = ps_weight[0]
    shard_rows = own_shard.shape[0]
    n_shard = lax.axis_size("shard")
    padded_width = shard_rows * n_shard
    in_width = x_rows.shape[1]
    x_padded = jnp.pad(x_rows, ((0, 0), (0, padded_width - in_width)))
    debiased = (own_shard / weight).astype(jnp.bfloat16)
    contract_cols = (((1,), (1,)), ((), ()))
    gathered = lax.all_gather(debiased, "shard", axis=0, tiled=True)
    pre_act = jnp.dot(x_padded, gathered, preferred_element_type=jnp.float32)
    sigmoid_pre = jax.nn.sigmoid(pre_act)
    d_pre = (
        up_rows.astype(jnp.float32) * sigmoid_pre * (1.0 + pre_act * (1.0 - sigmoid_pre))
    ).astype(jnp.bfloat16)
    back_full = lax.dot_general(d_pre, gathered, contract_cols, preferred_element_type=jnp.float32)
    grad_in = back_full[:, :in_width].astype(jnp.bfloat16)
    contract_rows = (((0,), (0,)), ((), ()))
    local_grad = lax.dot_general(x_padded, d_pre, contract_rows, preferred_element_type=jnp.float32)
    summed = lax.psum(local_grad.astype(jnp.bfloat16), "shard").astype(jnp.float32)
    my_rows = lax.dynamic_slice_in_dim(summed, lax.axis_index("shard") * shard_rows, shard_rows, 0)
    group_tokens = x_rows.shape[0] * n_shard
    stepped = own_shard - learn_rate * my_rows / group_tokens
    n_groups = lax.axis_size("gossip")
    levels = n_groups.bit_length() - 1
    distance = jnp.left_shift(jnp.int32(1), step[0] % levels)
    ordinal = jnp.arange(n_groups, dtype=jnp.int32)
    matches = cycle_order[:, None] == ordinal[None, :]
    position = jnp.sum(jnp.where(matches, ordinal[:, None], 0), axis=0)
    source_pos = (position - distance) % n_groups
    sources = jnp.sum(
        jnp.where(source_pos[:, None] == ordinal[None, :], cycle_order[None, :], 0), axis=1
    )
    flattened = stepped.reshape(n_groups, -1)
    weight_tiles = jnp.full((n_groups,), weight, jnp.float32)
    received, received_w = (
        lax.all_to_all(
            flattened.astype(jnp.bfloat16), "gossip", split_axis=0, concat_axis=0, tiled=True
        ).astype(flattened.dtype),
        lax.all_to_all(
            weight_tiles.astype(jnp.bfloat16), "gossip", split_axis=0, concat_axis=0, tiled=True
        ).astype(weight_tiles.dtype),
    )
    outgoing = jnp.take(received, sources, axis=0)
    outgoing_w = jnp.take(received_w, sources, axis=0)
    arrived, arrived_w = (
        lax.all_to_all(
            outgoing.astype(jnp.bfloat16), "gossip", split_axis=0, concat_axis=0, tiled=True
        ).astype(outgoing.dtype),
        lax.all_to_all(
            outgoing_w.astype(jnp.bfloat16), "gossip", split_axis=0, concat_axis=0, tiled=True
        ).astype(outgoing_w.dtype),
    )
    partner = arrived.reshape(stepped.shape)
    new_params = 0.5 * stepped + 0.5 * partner
    new_weight = 0.5 * weight + 0.5 * arrived_w[0]
    return (grad_in[None], new_params[None], jnp.reshape(new_weight, (1,)))


def solution(mesh):
    placed = (
        P("gossip", "shard", None),
        P("gossip", "shard", None),
        P("gossip", "shard", None),
        P("gossip"),
        P(),
        P(),
    )
    return jax.shard_map(
        body,
        mesh=mesh,
        in_specs=placed,
        out_specs=(P("gossip", "shard", None), P("gossip", "shard", None), P("gossip")),
        check_vma=False,
    )
```

profile of v0, /device:TPU:8, one launch (start us, length us, event | category | flops | bytes accessed | tf_op | source)
XLA Modules:
  0.0 442.8 jit_solution(7423503846964349468)
XLA Ops:
  7.9 1.6 fusion.9
  9.6 71.2 %all-gather.2.cloned.1.call-done = bf16[2048,1010]{1,0:T(8,128)(2,1)} async-done(((bf16[64,1010]{1,0:T(8,128)(2,1)}), bf16[2048,1010]{1,0:T(8,128)(2,1)}) %all-gather.2.cloned.1.call-update) | async-done | bytes 4136976 | tf_op jit(solution)/shard_map/all_gather | solution.py:21
  80.8 5.5 %fusion.2 = bf16[432,1010]{1,0:T(8,128)(2,1)S(1)} fusion(bf16[2048,1010]{1,0:T(8,128)(2,1)} %all-gather.2.cloned.1.call-done, bf16[432,2020]{1,0:T(8,128)(2,1)} %bitcast.53, bf16[1,432,1010]{2,1,0:T(8,128)(2,1)} %param.7), kind=kOutput, calls=%fused_computation.7 | convolution fusion | flops 1791530240 | bytes 7627520 | tf_op jit(solution)/shard_map/dot_general | solution.py:22
  86.3 4.4 convolution_convert_fusion
  90.7 0.6 broadcast_in_dim.56
  91.3 9.1 %all-to-all-start.2 = ((bf16[16,1,1]{2,1,0:T(2,128)(2,1)}), bf16[16,1,1]{2,1,0:T(2,128)(2,1)S(1)}, u32[]{:S(2)}, u32[]{:S(2)}) async-start(bf16[16,1,1]{2,1,0:T(2,128)(2,1)} %broadcast_in_dim.56), calls=%async_computation.2 | async-start | bytes 16384 | tf_op jit(solution)/shard_map/all_to_all | solution.py:51
  101.2 0.2 select_reduce_fusion
  101.4 6.1 %all-to-all-done.2 = bf16[16,1,1]{2,1,0:T(2,128)(2,1)S(1)} async-done(((bf16[16,1,1]{2,1,0:T(2,128)(2,1)}), bf16[16,1,1]{2,1,0:T(2,128)(2,1)S(1)}, u32[]{:S(2)}, u32[]{:S(2)}) %all-to-all-start.2) | async-done | bytes 64 | tf_op jit(solution)/shard_map/all_to_all | solution.py:51
  107.5 0.2 convert_reduce_fusion.1
  107.7 0.7 gather_fusion.1
  108.4 0.7 copy.20
  109.1 4.7 %all-to-all-start.3 = ((bf16[16,1,1]{2,1,0:T(2,128)(2,1)}), bf16[16,1,1]{2,1,0:T(2,128)(2,1)S(1)}, u32[]{:S(2)}, u32[]{:S(2)}) async-start(bf16[16,1,1]{2,1,0:T(2,128)(2,1)} %copy.20), calls=%async_computation.3 | async-start | bytes 16384 | tf_op jit(solution)/shard_map/all_to_all | solution.py:61
  113.8 7.3 %all-to-all-done.3 = bf16[16,1,1]{2,1,0:T(2,128)(2,1)S(1)} async-done(((bf16[16,1,1]{2,1,0:T(2,128)(2,1)}), bf16[16,1,1]{2,1,0:T(2,128)(2,1)S(1)}, u32[]{:S(2)}, u32[]{:S(2)}) %all-to-all-start.3) | async-done | bytes 64 | tf_op jit(solution)/shard_map/all_to_all | solution.py:61
  121.0 0.5 slice.16
  122.2 272.0 %all-reduce.3.cloned.1.call-done = bf16[2048,1010]{1,0:T(8,128)(2,1)} async-done(((bf16[2048,1010]{1,0:T(8,128)(2,1)}), bf16[2048,1010]{1,0:T(8,128)(2,1)}) %all-reduce.3.cloned.1.call-update) | async-done | bytes 4136976 | tf_op jit(solution)/shard_map/psum | solution.py:31
  394.2 0.9 fusion.10
  395.2 0.2 convert_element_type.100
  395.4 0.5 broadcast.159
  395.9 1.4 reduce.4
  397.4 0.8 reshape.158
  398.2 10.3 %all-to-all-start = ((bf16[16,2,2020]{2,1,0:T(2,128)(2,1)}), bf16[16,2,2020]{2,1,0:T(2,128)(2,1)S(1)}, u32[]{:S(2)}, u32[]{:S(2)}) async-start(bf16[16,2,2020]{2,1,0:T(2,128)(2,1)} %reshape.158), calls=%async_computation | async-start | bytes 262144 | tf_op jit(solution)/shard_map/all_to_all | solution.py:48
  408.6 4.2 fusion.16
  412.8 4.2 all-to-all-done
  417.0 0.2 reshape.159
  417.3 0.6 gather_fusion
  418.0 0.7 reduce.5
  418.7 0.8 reshape.160
  419.6 4.1 all-to-all-start.1
  423.6 1.3 fusion
  424.9 7.2 %all-to-all-done.1 = bf16[16,2,2020]{2,1,0:T(2,128)(2,1)S(1)} async-done(((bf16[16,2,2020]{2,1,0:T(2,128)(2,1)}), bf16[16,2,2020]{2,1,0:T(2,128)(2,1)S(1)}, u32[]{:S(2)}, u32[]{:S(2)}) %all-to-all-start.1) | async-done | bytes 129312 | tf_op jit(solution)/shard_map/all_to_all | solution.py:58
  432.3 0.7 convert_reduce_fusion
  433.1 1.7 multiply_bitcast_fusion
  (20 shorter events, 0.8 us)
Async XLA Ops:
  7.2 73.6 %all-gather.2.cloned.1.call-start = ((), (), s32[]{:S(2)}) async-start(), calls=%async_computation.4 | async-start | bytes 4325376 | tf_op jit(solution)/shard_map/all_gather | solution.py:21
  9.5 384.7 %all-reduce.3.cloned.1.call-start = ((), (), s32[]{:S(2)}) async-start(), calls=%async_computation.5 | async-start | bytes 8388608 | tf_op jit(solution)/shard_map/psum | solution.py:31
  80.8 5.5 %copy-start.1 = (bf16[1,432,2020]{2,1,0:T(8,128)(2,1)S(1)}, bf16[1,432,2020]{2,1,0:T(8,128)(2,1)}, u32[]{:S(2)}) copy-start(bf16[1,432,2020]{2,1,0:T(8,128)(2,1)} %param.6) | copy-start | bytes 5235844
  90.6 10.4 %copy-start.2 = (s32[16]{0:T(128)S(1)}, s32[16]{0:T(128)}, u32[]{:S(2)}) copy-start(s32[16]{0:T(128)} %param.11) | copy-start | bytes 196
  90.6 303.6 %copy-start = (f32[1,64,1010]{2,1,0:T(8,128)S(1)}, f32[1,64,1010]{2,1,0:T(8,128)}, u32[]{:S(2)}) copy-start(f32[1,64,1010]{2,1,0:T(8,128)} %param.8) | copy-start | bytes 775684
  91.3 16.2 %all-to-all-start.2 = ((bf16[16,1,1]{2,1,0:T(2,128)(2,1)}), bf16[16,1,1]{2,1,0:T(2,128)(2,1)S(1)}, u32[]{:S(2)}, u32[]{:S(2)}) async-start(bf16[16,1,1]{2,1,0:T(2,128)(2,1)} %broadcast_in_dim.56), calls=%async_computation.2 | async-start | bytes 16384 | tf_op jit(solution)/shard_map/all_to_all | solution.py:51
  109.1 12.0 %all-to-all-start.3 = ((bf16[16,1,1]{2,1,0:T(2,128)(2,1)}), bf16[16,1,1]{2,1,0:T(2,128)(2,1)S(1)}, u32[]{:S(2)}, u32[]{:S(2)}) async-start(bf16[16,1,1]{2,1,0:T(2,128)(2,1)} %copy.20), calls=%async_computation.3 | async-start | bytes 16384 | tf_op jit(solution)/shard_map/all_to_all | solution.py:61
  398.2 18.8 %all-to-all-start = ((bf16[16,2,2020]{2,1,0:T(2,128)(2,1)}), bf16[16,2,2020]{2,1,0:T(2,128)(2,1)S(1)}, u32[]{:S(2)}, u32[]{:S(2)}) async-start(bf16[16,2,2020]{2,1,0:T(2,128)(2,1)} %reshape.158), calls=%async_computation | async-start | bytes 262144 | tf_op jit(solution)/shard_map/all_to_all | solution.py:48
  419.6 12.5 %all-to-all-start.1 = ((bf16[16,2,2020]{2,1,0:T(2,128)(2,1)}), bf16[16,2,2020]{2,1,0:T(2,128)(2,1)S(1)}, u32[]{:S(2)}, u32[]{:S(2)}) async-start(bf16[16,2,2020]{2,1,0:T(2,128)(2,1)} %reshape.160), calls=%async_computation.1 | async-start | bytes 262144 | tf_op jit(solution)/shard_map/all_to_all | solution.py:58
Sparse Core Ops, SparseCore 0:
  11.7 69.0 all-gather.1
  90.8 303.4 all-reduce.2
where the time goes:
time: 443 us
  waiting for transfers between devices  368 us (83%)
  starting transfers between devices  28.3 us (6%)
  between operations  17.3 us (4%)
  matrix products  14.1 us (3%)
  other arithmetic  7.69 us (2%)
  local copies, waits for them, and re-layouts  7.46 us (2%)
    psum x1, waiting for transfers between devices, body(): lax.psum(local_grad.astype(jnp.bfloat16), 'shard').astype(jnp.float32)  272 us
    all_gather x1, waiting for transfers between devices, body(): gathered = lax.all_gather(debiased, 'shard', axis=0, tiled=True)  71.2 us
    all_to_all x1, starting transfers between devices, body(): lax.all_to_all(flattened.astype(jnp.bfloat16), 'gossip', split_axis=0, co...  10.3 us
    all_to_all x1, starting transfers between devices, body(): lax.all_to_all(weight_tiles.astype(jnp.bfloat16), 'gossip', split_axis=0,...  9.08 us
  transfers between devices with their start and end apart: 6, of which 6 were waited for; matrix products, arithmetic and copies ran while one was open for 2% of the time, Pallas kernels for 0%

commit v1 on v0

--- a/solution.py
+++ b/solution.py
@@ -18,7 +18,9 @@
     x_padded = jnp.pad(x_rows, ((0, 0), (0, padded_width - in_width)))
     debiased = (own_shard / weight).astype(jnp.bfloat16)
     contract_cols = (((1,), (1,)), ((), ()))
-    gathered = lax.all_gather(debiased, "shard", axis=0, tiled=True)
+    gathered = jnp.concatenate(
+        lax.all_to_all(jnp.stack([debiased] * lax.axis_size("shard")), "shard", 0, 0), axis=0
+    )
     pre_act = jnp.dot(x_padded, gathered, preferred_element_type=jnp.float32)
     sigmoid_pre = jax.nn.sigmoid(pre_act)
     d_pre = (

time: 443 us -> 479 us (1.081)
  blocking collectives: 0 us -> 89.2 us
  waiting for transfers between devices: 368 us -> 296 us
  starting transfers between devices: 28.3 us -> 48.2 us
    all_to_all x0 -> x1, blocking collectives: none -> 89.2 us  [body(): lax.all_to_all(jnp.stack([debiased] * lax.axis_size('shard')), 'shard', 0...]
    all_gather x1 -> x0, waiting for transfers between devices: 71.2 us -> none  [body(): gathered = lax.all_gather(debiased, 'shard', axis=0, tiled=True)]
    all_to_all x1, starting transfers between devices: 9.08 us -> 29.1 us  [body(): lax.all_to_all(weight_tiles.astype(jnp.bfloat16), 'gossip', split_axis=0,...]
  transfers between devices with their start and end apart: 6 -> 5, of which waited for: 6 -> 5; matrix products, arithmetic and copies ran while one was open for 2% -> 2% of each run, Pallas kernels for 0% -> 0%
where the time goes in v1:
time: 479 us; the launch traced here: 478 us
  waiting for transfers between devices  296 us (62%)
  blocking collectives  89.2 us (19%)
  starting transfers between devices  48.2 us (10%)
  between operations  17.3 us (4%)
  matrix products  11.1 us (2%)
  local copies, waits for them, and re-layouts  9.91 us (2%)
  other arithmetic  7 us (1%)
    psum x1, waiting for transfers between devices, body(): lax.psum(local_grad.astype(jnp.bfloat16), 'shard').astype(jnp.float32)  271 us
    all_to_all x1, blocking collectives, body(): lax.all_to_all(jnp.stack([debiased] * lax.axis_size('shard')), 'shard', 0...  89.2 us
    all_to_all x1, starting transfers between devices, body(): lax.all_to_all(weight_tiles.astype(jnp.bfloat16), 'gossip', split_axis=0,...  29.1 us
    all_to_all x1, starting transfers between devices, body(): lax.all_to_all(flattened.astype(jnp.bfloat16), 'gossip', split_axis=0, co...  10.3 us
  transfers between devices with their start and end apart: 5, of which 5 were waited for; matrix products, arithmetic and copies ran while one was open for 2% of the time, Pallas kernels for 0%

profile of v1, /device:TPU:8, one launch (start us, length us, event | category | flops | bytes accessed | tf_op | source)
XLA Modules:
  0.0 478.3 jit_solution(15681595358421870643)
XLA Ops:
  7.9 1.0 fusion.10
  8.8 0.5 stack.5
  9.4 89.2 %all_to_all.29 = bf16[32,64,1010]{2,1,0:T(8,128)(2,1)S(1)} all-to-all(bf16[32,64,1010]{2,1,0:T(8,128)(2,1)S(1)} %stack.5), channel_id=1, replica_groups=mesh['gossip'=16,'shard'=32] {'shard'}, dimensions={0} | all-to-all | bytes 8273920 | tf_op jit(solution)/shard_map/all_to_all | solution.py:22
  98.6 1.9 copy-done
  100.5 2.5 fusion.2
  103.0 4.4 convolution_convert_fusion
  107.4 0.6 broadcast_in_dim.56
  108.0 29.1 %all-to-all-start.3 = ((bf16[16,1,1]{2,1,0:T(2,128)(2,1)}), bf16[16,1,1]{2,1,0:T(2,128)(2,1)S(1)}, u32[]{:S(2)}, u32[]{:S(2)}) async-start(bf16[16,1,1]{2,1,0:T(2,128)(2,1)} %broadcast_in_dim.56), calls=%async_computation.3 | async-start | bytes 16384 | tf_op jit(solution)/shard_map/all_to_all | solution.py:53
  138.1 6.1 %all-to-all-done.3 = bf16[16,1,1]{2,1,0:T(2,128)(2,1)S(1)} async-done(((bf16[16,1,1]{2,1,0:T(2,128)(2,1)}), bf16[16,1,1]{2,1,0:T(2,128)(2,1)S(1)}, u32[]{:S(2)}, u32[]{:S(2)}) %all-to-all-start.3) | async-done | bytes 64 | tf_op jit(solution)/shard_map/all_to_all | solution.py:53
  144.2 0.2 convert_reduce_fusion.1
  144.4 0.7 gather_fusion.1
  145.1 0.7 copy.20
  145.8 4.7 all-to-all-start.4
  150.5 7.2 %all-to-all-done.4 = bf16[16,1,1]{2,1,0:T(2,128)(2,1)S(1)} async-done(((bf16[16,1,1]{2,1,0:T(2,128)(2,1)}), bf16[16,1,1]{2,1,0:T(2,128)(2,1)S(1)}, u32[]{:S(2)}, u32[]{:S(2)}) %all-to-all-start.4) | async-done | bytes 64 | tf_op jit(solution)/shard_map/all_to_all | solution.py:63
  157.7 0.5 slice.16
  158.8 271.0 %all-reduce.3.cloned.1.call-done = bf16[2048,1010]{1,0:T(8,128)(2,1)} async-done(((bf16[2048,1010]{1,0:T(8,128)(2,1)}), bf16[2048,1010]{1,0:T(8,128)(2,1)}) %all-reduce.3.cloned.1.call-update) | async-done | bytes 4136976 | tf_op jit(solution)/shard_map/psum | solution.py:33
  429.8 0.9 fusion.9
  430.8 0.2 convert_element_type.101
  431.0 0.5 broadcast.161
  431.5 1.4 reduce.4
  432.9 0.8 reshape.163
  433.8 10.3 %all-to-all-start.1 = ((bf16[16,2,2020]{2,1,0:T(2,128)(2,1)}), bf16[16,2,2020]{2,1,0:T(2,128)(2,1)S(1)}, u32[]{:S(2)}, u32[]{:S(2)}) async-start(bf16[16,2,2020]{2,1,0:T(2,128)(2,1)} %reshape.163), calls=%async_computation.1 | async-start | bytes 262144 | tf_op jit(solution)/shard_map/all_to_all | solution.py:50
  444.1 4.2 fusion.16
  448.3 4.2 all-to-all-done.1
  452.9 0.6 gather_fusion
  453.6 0.7 reduce.5
  454.3 0.8 reshape.165
  455.1 4.1 all-to-all-start.2
  459.2 1.3 fusion
  460.5 7.2 %all-to-all-done.2 = bf16[16,2,2020]{2,1,0:T(2,128)(2,1)S(1)} async-done(((bf16[16,2,2020]{2,1,0:T(2,128)(2,1)}), bf16[16,2,2020]{2,1,0:T(2,128)(2,1)S(1)}, u32[]{:S(2)}, u32[]{:S(2)}) %all-to-all-start.2) | async-done | bytes 129312 | tf_op jit(solution)/shard_map/all_to_all | solution.py:60
  467.8 0.7 convert_reduce_fusion
  468.7 1.7 multiply_bitcast_fusion
  (23 shorter events, 1.1 us)
Async XLA Ops:
  7.2 422.7 %all-reduce.3.cloned.1.call-start = ((), (), s32[]{:S(2)}) async-start(), calls=%async_computation.5 | async-start | bytes 8388608 | tf_op jit(solution)/shard_map/psum | solution.py:33
  9.4 91.2 %copy-start.2 = (bf16[1,432,2020]{2,1,0:T(8,128)(2,1)S(1)}, bf16[1,432,2020]{2,1,0:T(8,128)(2,1)}, u32[]{:S(2)}) copy-start(bf16[1,432,2020]{2,1,0:T(8,128)(2,1)} %param.6) | copy-start | bytes 5235844
  9.4 91.2 %copy-start.3 = (bf16[1,432,1010]{2,1,0:T(8,128)(2,1)S(1)}, bf16[1,432,1010]{2,1,0:T(8,128)(2,1)}, u32[]{:S(2)}) copy-start(bf16[1,432,1010]{2,1,0:T(8,128)(2,1)} %param.7) | copy-start | bytes 2617924
  98.6 1.9 copy-start
  107.4 30.4 %copy-start.4 = (s32[16]{0:T(128)S(1)}, s32[16]{0:T(128)}, u32[]{:S(2)}) copy-start(s32[16]{0:T(128)} %param.11) | copy-start | bytes 196
  107.4 322.4 %copy-start.1 = (f32[1,64,1010]{2,1,0:T(8,128)S(1)}, f32[1,64,1010]{2,1,0:T(8,128)}, u32[]{:S(2)}) copy-start(f32[1,64,1010]{2,1,0:T(8,128)} %param.8) | copy-start | bytes 775684
  108.0 36.2 %all-to-all-start.3 = ((bf16[16,1,1]{2,1,0:T(2,128)(2,1)}), bf16[16,1,1]{2,1,0:T(2,128)(2,1)S(1)}, u32[]{:S(2)}, u32[]{:S(2)}) async-start(bf16[16,1,1]{2,1,0:T(2,128)(2,1)} %broadcast_in_dim.56), calls=%async_computation.3 | async-start | bytes 16384 | tf_op jit(solution)/shard_map/all_to_all | solution.py:53
  145.8 11.9 %all-to-all-start.4 = ((bf16[16,1,1]{2,1,0:T(2,128)(2,1)}), bf16[16,1,1]{2,1,0:T(2,128)(2,1)S(1)}, u32[]{:S(2)}, u32[]{:S(2)}) async-start(bf16[16,1,1]{2,1,0:T(2,128)(2,1)} %copy.20), calls=%async_computation.4 | async-start | bytes 16384 | tf_op jit(solution)/shard_map/all_to_all | solution.py:63
  433.8 18.8 %all-to-all-start.1 = ((bf16[16,2,2020]{2,1,0:T(2,128)(2,1)}), bf16[16,2,2020]{2,1,0:T(2,128)(2,1)S(1)}, u32[]{:S(2)}, u32[]{:S(2)}) async-start(bf16[16,2,2020]{2,1,0:T(2,128)(2,1)} %reshape.163), calls=%async_computation.1 | async-start | bytes 262144 | tf_op jit(solution)/shard_map/all_to_all | solution.py:50
  455.1 12.5 %all-to-all-start.2 = ((bf16[16,2,2020]{2,1,0:T(2,128)(2,1)}), bf16[16,2,2020]{2,1,0:T(2,128)(2,1)S(1)}, u32[]{:S(2)}, u32[]{:S(2)}) async-start(bf16[16,2,2020]{2,1,0:T(2,128)(2,1)} %reshape.165), calls=%async_computation.2 | async-start | bytes 262144 | tf_op jit(solution)/shard_map/all_to_all | solution.py:60
Sparse Core Ops, SparseCore 0:
  107.5 322.2 all-reduce.2
